TPU v7x, 512 devices: a whole 4x4x16 slice. The times are simulated.
512 devices in a mesh: segment: 64 (over y, x, z_hi, core), fsdp: 8 (over z_lo).
Axes of the slice: x: 4, y: 4, z: 16 (z_hi: 2, z_lo: 8; z = z_hi * 8 + z_lo), core: 2. Of those that a mesh axis runs over, the one named last changes fastest.
Arguments:
- stream: bfloat16 [2, 64, 512, 4096], P(None, 'segment', 'fsdp'), may hold values from -60 to 60
- gain: bfloat16 [2, 64, 4096], P(None, 'segment'), may hold values from 0.099609375 to 1.8984375
- w_query: bfloat16 [2, 64, 32, 128, 128], P(None, 'segment', 'fsdp'), may hold values from -20 to 20
- w_key: bfloat16 [2, 64, 32, 128, 128], P(None, 'segment', 'fsdp'), may hold values from -20 to 20
- w_value: bfloat16 [2, 64, 32, 128, 128], P(None, 'segment', 'fsdp'), may hold values from -0.5 to 0.5
- w_mix: bfloat16 [2, 64, 128, 32, 32], P(None, 'segment', 'fsdp'), may hold values from -1 to 1
- active: int32 [2, 64], P(None, 'segment'), may hold values from 0 to 1
- random_blocks: int32 [2, 64, 8, 2], P(None, 'segment'), may hold values from 0 to 7
Outputs:
- advanced: bfloat16 [2, 64, 512, 4096], P(None, 'segment', 'fsdp')
All inputs are finite; a program needn't handle non-finite values.
Results may differ from a plain program's by a relative error of at most 0.009.
Values may be sent and summed in bfloat16 or wider, within the bound.
No kernel may reach another device: no remote copies, remote signals or barrier semaphores. Data moves between devices by JAX's collectives and lax.ppermute only.
A program may use at most 64 MiB of HBM per device.

v0:
```python
import jax
import jax.numpy as jnp
from jax import lax
from jax.sharding import PartitionSpec as P

BLK = 64
ROUNDS = 2
EPS = 1e-05


def shifted(value, axis, by):
    devices = lax.axis_size(axis)
    return lax.ppermute(value, axis, [(i, (i + by) % devices) for i in range(devices)])


def block_attention(query, keys, values, random_ids):
    heads, seq_len, head_width = query.shape
    count = seq_len // BLK
    query_blocks = query.reshape(heads, count, BLK, head_width)
    key_blocks = keys.reshape(heads, count, BLK, head_width)
    value_blocks = values.reshape(heads, count, BLK, head_width)
    block_ids = jnp.arange(count, dtype=jnp.int32)
    window = jnp.stack(
        [(block_ids - 1) % count, block_ids, (block_ids + 1) % count, jnp.zeros_like(block_ids)],
        axis=1,
    )
    chosen = jnp.concatenate([window, random_ids], axis=1)
    picked_keys = key_blocks[:, chosen].reshape(heads, count, chosen.shape[1] * BLK, head_width)
    picked_values = value_blocks[:, chosen].reshape(heads, count, chosen.shape[1] * BLK, head_width)
    scores = jnp.einsum(
        "hnqd,hnkd->hnqk", query_blocks, picked_keys, preferred_element_type=jnp.float32
    )
    row_max = jnp.max(scores, axis=-1, keepdims=True)
    powers = jnp.exp(scores - row_max)
    weights = (powers / jnp.sum(powers, axis=-1, keepdims=True)).astype(jnp.bfloat16)
    mixed = jnp.einsum(
        "hnqk,hnkd->hnqd", weights, picked_values, preferred_element_type=jnp.float32
    ).astype(jnp.bfloat16)
    return mixed.reshape(heads, seq_len, head_width)


def head_attention(view, queries_w, keys_w, values_w, random_ids):

    def one_segment(items):
        rows, weight_q, weight_k, weight_v, ids = items
        raw = jnp.einsum("thc,hcd->htd", rows, weight_q, preferred_element_type=jnp.float32)
        query = (raw * rows.shape[-1] ** (-0.5)).astype(jnp.bfloat16)
        keys = jnp.einsum(
            "thc,hcd->htd", rows, weight_k, preferred_element_type=jnp.float32
        ).astype(jnp.bfloat16)
        values = jnp.einsum(
            "thc,hcd->htd", rows, weight_v, preferred_element_type=jnp.float32
        ).astype(jnp.bfloat16)
        return block_attention(query, keys, values, ids)

    return lax.map(one_segment, (view, queries_w, keys_w, values_w, random_ids))


def mix_heads(attended, mix_w):
    return jnp.einsum(
        "vhtc,vchg->vtgc",
        attended,
        lax.all_gather(mix_w, "fsdp", axis=1, tiled=True),
        preferred_element_type=jnp.float32,
    ).astype(jnp.bfloat16)


def cycle(values):
    moved = shifted(values, "segment", 1)
    return jnp.where(lax.axis_index("segment") == 0, jnp.roll(moved, 1, axis=0), moved)


def token_layer(state, params):
    queries_w, keys_w, values_w, mix_w, gains, live, random_ids = params
    wide = state.astype(jnp.float32)
    mean_sq = jnp.mean(wide * wide, axis=2, keepdims=True)
    normed = (wide * lax.rsqrt(mean_sq + EPS) * gains[:, None, :].astype(jnp.float32)).astype(
        jnp.bfloat16
    )
    view = normed.reshape(state.shape[0], state.shape[1], -1, queries_w.shape[-1])
    gathered = lax.all_to_all(view, "fsdp", split_axis=2, concat_axis=1, tiled=True)
    attended = head_attention(gathered, queries_w, keys_w, values_w, random_ids)
    returned = lax.all_to_all(attended, "fsdp", split_axis=2, concat_axis=1, tiled=True)
    mixed = mix_heads(returned, mix_w)
    updated = (wide + mixed.reshape(wide.shape).astype(jnp.float32)).astype(jnp.bfloat16)
    return jnp.where(live[:, None, None] > 0, updated, state)


def shards(stream, gain, w_query, w_key, w_value, w_mix, active, random_blocks):
    params = (
        w_query[:, 0],
        w_key[:, 0],
        w_value[:, 0],
        w_mix[:, 0],
        gain[:, 0],
        active[:, 0],
        random_blocks[:, 0],
    )
    state = stream[:, 0]
    for round_index in range(ROUNDS):
        state = token_layer(state, params)
        state = cycle(state)
    return state[:, None]


def solution(mesh):
    in_specs = (
        P(None, "segment", "fsdp", None),
        P(None, "segment", None),
        P(None, "segment", "fsdp", None, None),
        P(None, "segment", "fsdp", None, None),
        P(None, "segment", "fsdp", None, None),
        P(None, "segment", "fsdp", None, None),
        P(None, "segment"),
        P(None, "segment", None, None),
    )
    out_specs = P(None, "segment", "fsdp", None)
    return jax.shard_map(shards, mesh=mesh, in_specs=in_specs, out_specs=out_specs, check_vma=False)
```

profile of v0, /device:TPU:32, one launch (start us, length us, event | category | flops | bytes accessed | tf_op | source)
XLA Modules:
  0.0 546.5 jit_solution(105183954423557872)
XLA Ops:
  5.5 12.8 %all-to-all-start = ((bf16[2,64,32,128]{3,1,0,2:T(8,128)(2,1)}), bf16[2,64,32,128]{3,1,0,2:T(8,128)(2,1)S(1)}, u32[]{:S(2)}, u32[]{:S(2)}) async-start(bf16[2,64,32,128]{3,1,0,2:T(8,128)(2,1)} %copy.69), calls=%async_computation | async-start | bytes 2097152 | tf_op jit(solution)/shard_map/all_to_all | solution.py:81
  18.3 48.3 %all-to-all-done = bf16[2,64,32,128]{3,1,0,2:T(8,128)(2,1)S(1)} async-done(((bf16[2,64,32,128]{3,1,0,2:T(8,128)(2,1)}), bf16[2,64,32,128]{3,1,0,2:T(8,128)(2,1)S(1)}, u32[]{:S(2)}, u32[]{:S(2)}) %all-to-all-start) | async-done | bytes 1048608 | tf_op jit(solution)/shard_map/all_to_all | solution.py:81
  68.9 56.5 %while.24 = (s32[]{:T(128)}, bf16[2,4,512,128]{3,1,0,2:T(4,128)(2,1)}, bf16[2,512,4,128]{3,1,2,0:T(8,128)(2,1)}, bf16[2,4,128,128]{3,2,1,0:T(8,128)(2,1)S(1)}, b...) while((s32[]{:T(128)}, ...), condition=%wide.region_4.5_spmd, body=%wide.region_1.4_spmd.sunk | while | flops 609226816 | bytes 59140032 | solution.py:56
  73.3 2.9 copy.106
  82.0 2.7 gather_fusion
  84.8 2.9 copy.105
  87.6 7.3 %fusion.139 = bf16[4,8,64,128]{3,2,1,0:T(8,128)(2,1)} fusion(bf16[4,8,384,128]{3,2,1,0:T(8,128)(2,1)S(1)} %bitcast.258, f32[4,8,64]{2,1,0:T(8,128)S(1)} %fusion.138, f32[4,8,64,384]{3,2,1,0:T(8,128)} %copy-done), kind=kOutput, calls=%fused_computation.9.clone.1 | convolution fusion | flops 203950464 | bytes 6823936 | tf_op jit(solution)/shard_map/while/body/eval_jaxpr/hnqk,hnkd->hnqd/dot_general | solution.py:36
  101.5 2.9 copy.106
  110.3 2.7 gather_fusion
  113.0 2.9 copy.105
  115.9 7.3 %fusion.139 = bf16[4,8,64,128]{3,2,1,0:T(8,128)(2,1)} fusion(bf16[4,8,384,128]{3,2,1,0:T(8,128)(2,1)S(1)} %bitcast.258, f32[4,8,64]{2,1,0:T(8,128)S(1)} %fusion.138, f32[4,8,64,384]{3,2,1,0:T(8,128)} %copy-done), kind=kOutput, calls=%fused_computation.9.clone.1 | convolution fusion | flops 203950464 | bytes 6823936 | tf_op jit(solution)/shard_map/while/body/eval_jaxpr/hnqk,hnkd->hnqd/dot_general | solution.py:36
  125.4 7.2 %all-to-all-start.1 = ((bf16[2,4,512,128]{3,1,0,2:T(4,128)(2,1)}), bf16[2,4,512,128]{3,1,0,2:T(4,128)(2,1)S(1)}, u32[]{:S(2)}, u32[]{:S(2)}) async-start(bf16[2,4,512,128]{3,1,0,2:T(4,128)(2,1)} %get-tuple-element.187), calls=%async_computation.1 | async-start | bytes 2097152 | tf_op jit(solution)/shard_map/all_to_all | solution.py:83
  134.4 89.3 %all-gather = bf16[2,1,128,32,32]{3,4,2,0,1:T(8,128)(2,1)S(1)} all-gather(bf16[2,1,16,32,32]{3,4,2,0,1:T(8,128)(2,1)} %copy.74), channel_id=2, replica_groups=mesh['segment'=64,'fsdp'=8] {'fsdp'}, dimensions={2}, use_global_device_ids=true | all-gather | bytes 589824 | tf_op jit(solution)/shard_map/all_gather | solution.py:63
  223.7 3.3 copy.73
  227.0 4.2 convert_bitcast_fusion.1
  231.2 5.3 copy.75
  241.7 51.0 %collective-permute-done = bf16[2,64,4096]{2,1,0:T(8,128)(2,1)S(1)} collective-permute-done((bf16[2,64,4096]{2,1,0:T(8,128)(2,1)}, bf16[2,64,4096]{2,1,0:T(8,128)(2,1)S(1)}, u32[]{:S(2)}, u32[]{:S(2)}) %collective-permute-start) | collective-permute-done | bytes 1048608 | tf_op jit(solution)/shard_map/ppermute | solution.py:13
  295.6 19.6 %all-to-all-start.2 = ((bf16[2,64,32,128]{3,1,0,2:T(8,128)(2,1)}), bf16[2,64,32,128]{3,1,0,2:T(8,128)(2,1)S(1)}, u32[]{:S(2)}, u32[]{:S(2)}) async-start(bf16[2,64,32,128]{3,1,0,2:T(8,128)(2,1)} %copy_bitcast_fusion), calls=%async_computation.2 | async-start | bytes 2097152 | tf_op jit(solution)/shard_map/all_to_all | solution.py:81
  315.2 38.3 %all-to-all-done.2 = bf16[2,64,32,128]{3,1,0,2:T(8,128)(2,1)S(1)} async-done(((bf16[2,64,32,128]{3,1,0,2:T(8,128)(2,1)}), bf16[2,64,32,128]{3,1,0,2:T(8,128)(2,1)S(1)}, u32[]{:S(2)}, u32[]{:S(2)}) %all-to-all-start.2) | async-done | bytes 1048608 | tf_op jit(solution)/shard_map/all_to_all | solution.py:81
  355.8 56.6 %while.25 = (s32[]{:T(128)}, bf16[2,4,512,128]{3,1,0,2:T(4,128)(2,1)}, bf16[2,512,4,128]{3,1,2,0:T(8,128)(2,1)}, bf16[2,4,128,128]{3,2,1,0:T(8,128)(2,1)S(1)}, b...) while((s32[]{:T(128)}, ...), condition=%wide.region_9.10_spmd, body=%wide.region_6.9_spmd.sunk | while | flops 609226816 | bytes 59140032 | solution.py:56
  360.1 2.9 copy.110
  371.6 2.9 copy.109
  374.5 7.3 %fusion.156 = bf16[4,8,64,128]{3,2,1,0:T(8,128)(2,1)} fusion(bf16[4,8,384,128]{3,2,1,0:T(8,128)(2,1)S(1)} %bitcast.259, f32[4,8,64]{2,1,0:T(8,128)S(1)} %fusion.155, f32[4,8,64,384]{3,2,1,0:T(8,128)} %copy-done.1), kind=kOutput, calls=%fused_computation.49.clone.1 | convolution fusion | flops 203950464 | bytes 6823936 | tf_op jit(solution)/shard_map/while/body/eval_jaxpr/hnqk,hnkd->hnqd/dot_general | solution.py:36
  388.4 2.9 copy.110
  397.2 2.7 gather_fusion.2
  399.9 2.9 copy.109
  402.8 7.3 %fusion.156 = bf16[4,8,64,128]{3,2,1,0:T(8,128)(2,1)} fusion(bf16[4,8,384,128]{3,2,1,0:T(8,128)(2,1)S(1)} %bitcast.259, f32[4,8,64]{2,1,0:T(8,128)S(1)} %fusion.155, f32[4,8,64,384]{3,2,1,0:T(8,128)} %copy-done.1), kind=kOutput, calls=%fused_computation.49.clone.1 | convolution fusion | flops 203950464 | bytes 6823936 | tf_op jit(solution)/shard_map/while/body/eval_jaxpr/hnqk,hnkd->hnqd/dot_general | solution.py:36
  412.4 55.1 %all_to_all.72 = bf16[2,4,512,128]{3,1,0,2:T(4,128)(2,1)S(1)} all-to-all(bf16[2,4,512,128]{3,1,0,2:T(4,128)(2,1)} %get-tuple-element.188), channel_id=1, replica_groups=mesh['segment'=64,'fsdp'=8] {'fsdp'}, dimensions={2} | all-to-all | bytes 2097152 | tf_op jit(solution)/shard_map/all_to_all | solution.py:83
  467.5 3.2 copy.79
  470.7 4.2 convert_bitcast_fusion
  474.9 4.5 copy.80
  484.9 60.4 %collective-permute-done.1 = bf16[2,64,4096]{2,1,0:T(8,128)(2,1)S(1)} collective-permute-done((bf16[2,64,4096]{2,1,0:T(8,128)(2,1)S(1)}, bf16[2,64,4096]{2,1,0:T(8,128)(2,1)S(1)}, u32[]{:S(2)}, u32[]{:S(2)}) %collective-permute-start.1) | collective-permute-done | bytes 1048608 | tf_op jit(solution)/shard_map/ppermute | solution.py:13
  (115 shorter events, 78.9 us)
Async XLA Ops:
  5.5 63.4 %copy-start.7 = (bf16[2,1,4,128,128]{4,3,2,1,0:T(8,128)(2,1)S(1)}, bf16[2,1,4,128,128]{4,3,2,1,0:T(8,128)(2,1)}, u32[]{:S(2)}) copy-start(bf16[2,1,4,128,128]{4,3,2,1,0:T(8,128)(2,1)} %param.14) | copy-start | bytes 786436
  5.5 63.4 %copy-start.8 = (s32[2,1,8,2]{2,3,1,0:T(2,128)S(1)}, s32[2,1,8,2]{2,3,1,0:T(2,128)}, u32[]{:S(2)}) copy-start(s32[2,1,8,2]{2,3,1,0:T(2,128)} %param.19) | copy-start | bytes 388
  5.5 61.1 %all-to-all-start = ((bf16[2,64,32,128]{3,1,0,2:T(8,128)(2,1)}), bf16[2,64,32,128]{3,1,0,2:T(8,128)(2,1)S(1)}, u32[]{:S(2)}, u32[]{:S(2)}) async-start(bf16[2,64,32,128]{3,1,0,2:T(8,128)(2,1)} %copy.69), calls=%async_computation | async-start | bytes 2097152 | tf_op jit(solution)/shard_map/all_to_all | solution.py:81
  68.9 65.4 %copy-start.9 = (s32[2,1]{0,1:T(1,128)S(1)}, s32[2,1]{0,1:T(1,128)}, u32[]{:S(2)}) copy-start(s32[2,1]{0,1:T(1,128)} %param.18) | copy-start | bytes 28
  79.0 1.7 copy-start
  107.3 1.7 copy-start
  125.4 98.2 %all-to-all-start.1 = ((bf16[2,4,512,128]{3,1,0,2:T(4,128)(2,1)}), bf16[2,4,512,128]{3,1,0,2:T(4,128)(2,1)S(1)}, u32[]{:S(2)}, u32[]{:S(2)}) async-start(bf16[2,4,512,128]{3,1,0,2:T(4,128)(2,1)} %get-tuple-element.187), calls=%async_computation.1 | async-start | bytes 2097152 | tf_op jit(solution)/shard_map/all_to_all | solution.py:83
  223.7 7.6 %copy-start.2 = (bf16[2,1,128,32,32]{3,4,2,0,1:T(8,128)(2,1)}, bf16[2,1,128,32,32]{3,4,2,0,1:T(8,128)(2,1)S(1)}, u32[]{:S(2)}) copy-start(bf16[2,1,128,32,32]{3,4,2,0,1:T(8,128)(2,1)S(1)} %all-gather) | copy-start | bytes 1572868
  236.5 1.9 copy-start.4
  239.8 52.9 %collective-permute-start = (bf16[2,64,4096]{2,1,0:T(8,128)(2,1)}, bf16[2,64,4096]{2,1,0:T(8,128)(2,1)S(1)}, u32[]{:S(2)}, u32[]{:S(2)}) collective-permute-start(bf16[2,64,4096]{2,1,0:T(8,128)(2,1)} %fusion.67), channel_id=1, source_target_pairs={{0,8},{8,16},{16,24},{24,32},{32,40},{40,48},{48,56},{56,64},{64,7... | collective-permute-start | bytes 3145736 | tf_op jit(solution)/shard_map/ppermute | solution.py:13
  293.2 1.0 copy-start.5
  295.6 57.8 %all-to-all-start.2 = ((bf16[2,64,32,128]{3,1,0,2:T(8,128)(2,1)}), bf16[2,64,32,128]{3,1,0,2:T(8,128)(2,1)S(1)}, u32[]{:S(2)}, u32[]{:S(2)}) async-start(bf16[2,64,32,128]{3,1,0,2:T(8,128)(2,1)} %copy_bitcast_fusion), calls=%async_computation.2 | async-start | bytes 2097152 | tf_op jit(solution)/shard_map/all_to_all | solution.py:81
  365.9 1.7 copy-start.1
  394.2 1.7 copy-start.1
  412.4 58.3 %copy-start.3 = (bf16[2,1,128,32,32]{3,4,2,0,1:T(8,128)(2,1)S(1)}, bf16[2,1,128,32,32]{3,4,2,0,1:T(8,128)(2,1)}, u32[]{:S(2)}) copy-start(bf16[2,1,128,32,32]{3,4,2,0,1:T(8,128)(2,1)} %copy-done.2) | copy-start | bytes 1572868
  479.4 1.6 copy-start.6
  483.0 62.3 %collective-permute-start.1 = (bf16[2,64,4096]{2,1,0:T(8,128)(2,1)S(1)}, bf16[2,64,4096]{2,1,0:T(8,128)(2,1)S(1)}, u32[]{:S(2)}, u32[]{:S(2)}) collective-permute-start(bf16[2,64,4096]{2,1,0:T(8,128)(2,1)S(1)} %fusion.66), channel_id=1, source_target_pairs={{0,8},{8,16},{16,24},{24,32},{32,40},{40,48},{48,56},{56,64},{64,7... | collective-permute-start | bytes 3145736 | tf_op jit(solution)/shard_map/ppermute | solution.py:13
where the time goes:
time: 548 us; the launch traced here: 547 us
  waiting for transfers between devices  198 us (36%)
  blocking collectives  144 us (26%)
  local copies, waits for them, and re-layouts  85.7 us (16%)
  matrix products  59.8 us (11%)
  starting transfers between devices  43.3 us (8%)
  other arithmetic  14.7 us (3%)
    ppermute x2, waiting for transfers between devices, shifted(): lax.ppermute(value, axis, [(i, (i + by) % devices) for i in range(devices)])  111 us
    all_gather x1, blocking collectives, mix_heads(): lax.all_gather(mix_w, 'fsdp', axis=1, tiled=True)  89.3 us
    all_to_all x2, waiting for transfers between devices, token_layer(): lax.all_to_all(view, 'fsdp', split_axis=2, concat_axis=1, tiled=True)  86.6 us
    all_to_all x1, blocking collectives, token_layer(): lax.all_to_all(attended, 'fsdp', split_axis=2, concat_axis=1, tiled=True)  55.1 us
    all_to_all x2, starting transfers between devices, token_layer(): lax.all_to_all(view, 'fsdp', split_axis=2, concat_axis=1, tiled=True)  32.4 us
    dot_general x4, matrix products, block_attention(): jnp.einsum('hnqk,hnkd->hnqd', weights, picked_values, preferred_element_t...  29.3 us
    gather x8, local copies, waits for them, and re-layouts, block_attention(): value_blocks[:, chosen]  22.4 us
    gather x8, local copies, waits for them, and re-layouts, block_attention(): key_blocks[:, chosen]  22.3 us
  transfers between devices with their start and end apart: 5, of which 4 were waited for; matrix products, arithmetic and copies ran while one was open for 0% of the time, Pallas kernels for 0%

commit v1 on v0

--- a/solution.py
+++ b/solution.py
@@ -60,7 +60,9 @@
     return jnp.einsum(
         "vhtc,vchg->vtgc",
         attended,
-        lax.all_gather(mix_w, "fsdp", axis=1, tiled=True),
+        jnp.concatenate(
+            lax.all_to_all(jnp.stack([mix_w] * lax.axis_size("fsdp")), "fsdp", 0, 0), axis=1
+        ),
         preferred_element_type=jnp.float32,
     ).astype(jnp.bfloat16)
 

time: 548 us -> 512 us (0.934)
  blocking collectives: 144 us -> 55.1 us
  waiting for transfers between devices: 198 us -> 238 us
  starting transfers between devices: 43.3 us -> 51.8 us
    all_gather x1 -> x0, blocking collectives: 89.3 us -> none  [mix_heads(): lax.all_gather(mix_w, 'fsdp', axis=1, tiled=True)]
    all_to_all x1, waiting for transfers between devices: 0.01 us -> 44 us  [token_layer(): lax.all_to_all(attended, 'fsdp', split_axis=2, concat_axis=1, tiled=True)]
    all_to_all x0 -> x1, starting transfers between devices: none -> 7.16 us  [mix_heads(): lax.all_to_all(jnp.stack([mix_w] * lax.axis_size('fsdp')), 'fsdp', 0, 0)]
  transfers between devices with their start and end apart: 5 -> 6, of which waited for: 4 -> 5; matrix products, arithmetic and copies ran while one was open for 0% -> 13% of each run, Pallas kernels for 0% -> 0%
where the time goes in v1:
time: 512 us; the launch traced here: 511 us
  waiting for transfers between devices  238 us (46%)
  local copies, waits for them, and re-layouts  91 us (18%)
  matrix products  59.8 us (12%)
  blocking collectives  55.1 us (11%)
  starting transfers between devices  51.8 us (10%)
  other arithmetic  14.7 us (3%)
    ppermute x2, waiting for transfers between devices, shifted(): lax.ppermute(value, axis, [(i, (i + by) % devices) for i in range(devices)])  110 us
    all_to_all x2, waiting for transfers between devices, token_layer(): lax.all_to_all(view, 'fsdp', split_axis=2, concat_axis=1, tiled=True)  83.7 us
    all_to_all x1, blocking collectives, token_layer(): lax.all_to_all(attended, 'fsdp', split_axis=2, concat_axis=1, tiled=True)  55.1 us
    all_to_all x1, waiting for transfers between devices, token_layer(): lax.all_to_all(attended, 'fsdp', split_axis=2, concat_axis=1, tiled=True)  44 us
    all_to_all x2, starting transfers between devices, token_layer(): lax.all_to_all(view, 'fsdp', split_axis=2, concat_axis=1, tiled=True)  30.9 us
    dot_general x4, matrix products, block_attention(): jnp.einsum('hnqk,hnkd->hnqd', weights, picked_values, preferred_element_t...  29.3 us
    gather x8, local copies, waits for them, and re-layouts, block_attention(): value_blocks[:, chosen]  22.4 us
    gather x8, local copies, waits for them, and re-layouts, block_attention(): key_blocks[:, chosen]  22.4 us
  transfers between devices with their start and end apart: 6, of which 5 were waited for; matrix products, arithmetic and copies ran while one was open for 13% of the time, Pallas kernels for 0%

profile of v1, /device:TPU:32, one launch (start us, length us, event | category | flops | bytes accessed | tf_op | source)
XLA Modules:
  0.0 510.6 jit_solution(4072898314802990096)
XLA Ops:
  5.5 12.6 %all-to-all-start = ((bf16[2,64,32,128]{3,1,0,2:T(8,128)(2,1)}), bf16[2,64,32,128]{3,1,0,2:T(8,128)(2,1)S(1)}, u32[]{:S(2)}, u32[]{:S(2)}) async-start(bf16[2,64,32,128]{3,1,0,2:T(8,128)(2,1)} %copy.69), calls=%async_computation | async-start | bytes 2097152 | tf_op jit(solution)/shard_map/all_to_all | solution.py:83
  21.5 45.0 %all-to-all-done = bf16[2,64,32,128]{3,1,0,2:T(8,128)(2,1)S(1)} async-done(((bf16[2,64,32,128]{3,1,0,2:T(8,128)(2,1)}), bf16[2,64,32,128]{3,1,0,2:T(8,128)(2,1)S(1)}, u32[]{:S(2)}, u32[]{:S(2)}) %all-to-all-start) | async-done | bytes 1048608 | tf_op jit(solution)/shard_map/all_to_all | solution.py:83
  66.5 7.2 %all-to-all-start.2 = ((bf16[8,2,16384]{2,1,0:T(2,128)(2,1)}), bf16[8,2,16384]{2,1,0:T(2,128)(2,1)}, u32[]{:S(2)}, u32[]{:S(2)}) async-start(bf16[8,2,16384]{2,1,0:T(2,128)(2,1)} %reshape.600), calls=%async_computation.2 | async-start | bytes 1048576 | tf_op jit(solution)/shard_map/all_to_all | solution.py:64
  76.0 56.5 %while.24 = (s32[]{:T(128)}, bf16[2,4,512,128]{3,1,0,2:T(4,128)(2,1)}, bf16[2,512,4,128]{3,1,2,0:T(8,128)(2,1)}, bf16[2,4,128,128]{3,2,1,0:T(8,128)(2,1)S(1)}, b...) while((s32[]{:T(128)}, ...), condition=%wide.region_4.5_spmd, body=%wide.region_1.4_spmd.sunk | while | flops 609226816 | bytes 59140032 | solution.py:56
  80.3 2.9 copy.107
  91.8 2.9 copy.106
  94.7 7.3 %fusion.133 = bf16[4,8,64,128]{3,2,1,0:T(8,128)(2,1)} fusion(bf16[4,8,384,128]{3,2,1,0:T(8,128)(2,1)S(1)} %bitcast.259, f32[4,8,64]{2,1,0:T(8,128)S(1)} %fusion.132, f32[4,8,64,384]{3,2,1,0:T(8,128)} %copy-done), kind=kOutput, calls=%fused_computation.9.clone.1 | convolution fusion | flops 203950464 | bytes 6823936 | tf_op jit(solution)/shard_map/while/body/eval_jaxpr/hnqk,hnkd->hnqd/dot_general | solution.py:36
  108.5 2.9 copy.107
  120.0 2.9 copy.106
  122.9 7.3 %fusion.133 = bf16[4,8,64,128]{3,2,1,0:T(8,128)(2,1)} fusion(bf16[4,8,384,128]{3,2,1,0:T(8,128)(2,1)S(1)} %bitcast.259, f32[4,8,64]{2,1,0:T(8,128)S(1)} %fusion.132, f32[4,8,64,384]{3,2,1,0:T(8,128)} %copy-done), kind=kOutput, calls=%fused_computation.9.clone.1 | convolution fusion | flops 203950464 | bytes 6823936 | tf_op jit(solution)/shard_map/while/body/eval_jaxpr/hnqk,hnkd->hnqd/dot_general | solution.py:36
  132.5 9.9 %all-to-all-start.1 = ((bf16[2,4,512,128]{3,1,0,2:T(4,128)(2,1)}), bf16[2,4,512,128]{3,1,0,2:T(4,128)(2,1)S(1)}, u32[]{:S(2)}, u32[]{:S(2)}) async-start(bf16[2,4,512,128]{3,1,0,2:T(4,128)(2,1)} %get-tuple-element.187), calls=%async_computation.1 | async-start | bytes 2097152 | tf_op jit(solution)/shard_map/all_to_all | solution.py:85
  142.4 3.1 reshape.601
  146.4 44.0 %all-to-all-done.1 = bf16[2,4,512,128]{3,1,0,2:T(4,128)(2,1)S(1)} async-done(((bf16[2,4,512,128]{3,1,0,2:T(4,128)(2,1)}), bf16[2,4,512,128]{3,1,0,2:T(4,128)(2,1)S(1)}, u32[]{:S(2)}, u32[]{:S(2)}) %all-to-all-start.1) | async-done | bytes 1048608 | tf_op jit(solution)/shard_map/all_to_all | solution.py:85
  190.3 3.2 copy.73
  193.5 4.2 convert_bitcast_fusion.1
  197.7 5.3 %copy.76 = f32[2,64,32,128]{3,2,1,0:T(8,128)} copy(f32[2,64,32,128]{1,2,3,0:T(8,128)} %convert_bitcast_fusion.1) | data formatting | bytes 4194304 | tf_op jit(solution)/shard_map/convert_element_type | solution.py:87
  208.2 49.9 %collective-permute-done = bf16[2,64,4096]{2,1,0:T(8,128)(2,1)S(1)} collective-permute-done((bf16[2,64,4096]{2,1,0:T(8,128)(2,1)}, bf16[2,64,4096]{2,1,0:T(8,128)(2,1)S(1)}, u32[]{:S(2)}, u32[]{:S(2)}) %collective-permute-start) | collective-permute-done | bytes 1048608 | tf_op jit(solution)/shard_map/ppermute | solution.py:13
  261.1 18.3 %all-to-all-start.3 = ((bf16[2,64,32,128]{3,1,0,2:T(8,128)(2,1)}), bf16[2,64,32,128]{3,1,0,2:T(8,128)(2,1)S(1)}, u32[]{:S(2)}, u32[]{:S(2)}) async-start(bf16[2,64,32,128]{3,1,0,2:T(8,128)(2,1)} %copy_bitcast_fusion), calls=%async_computation.3 | async-start | bytes 2097152 | tf_op jit(solution)/shard_map/all_to_all | solution.py:83
  279.4 38.7 %all-to-all-done.3 = bf16[2,64,32,128]{3,1,0,2:T(8,128)(2,1)S(1)} async-done(((bf16[2,64,32,128]{3,1,0,2:T(8,128)(2,1)}), bf16[2,64,32,128]{3,1,0,2:T(8,128)(2,1)S(1)}, u32[]{:S(2)}, u32[]{:S(2)}) %all-to-all-start.3) | async-done | bytes 1048608 | tf_op jit(solution)/shard_map/all_to_all | solution.py:83
  320.4 56.6 %while.25 = (s32[]{:T(128)}, bf16[2,4,512,128]{3,1,0,2:T(4,128)(2,1)}, bf16[2,512,4,128]{3,1,2,0:T(8,128)(2,1)}, bf16[2,4,128,128]{3,2,1,0:T(8,128)(2,1)S(1)}, b...) while((s32[]{:T(128)}, ...), condition=%wide.region_9.10_spmd, body=%wide.region_6.9_spmd.sunk | while | flops 609226816 | bytes 59140032 | solution.py:56
  324.7 2.9 copy.111
  333.5 2.7 gather_fusion.2
  336.2 2.9 copy.110
  339.1 7.3 %fusion.150 = bf16[4,8,64,128]{3,2,1,0:T(8,128)(2,1)} fusion(bf16[4,8,384,128]{3,2,1,0:T(8,128)(2,1)S(1)} %bitcast.260, f32[4,8,64]{2,1,0:T(8,128)S(1)} %fusion.149, f32[4,8,64,384]{3,2,1,0:T(8,128)} %copy-done.1), kind=kOutput, calls=%fused_computation.49.clone.1 | convolution fusion | flops 203950464 | bytes 6823936 | tf_op jit(solution)/shard_map/while/body/eval_jaxpr/hnqk,hnkd->hnqd/dot_general | solution.py:36
  353.1 2.9 copy.111
  364.5 2.9 copy.110
  367.4 7.3 %fusion.150 = bf16[4,8,64,128]{3,2,1,0:T(8,128)(2,1)} fusion(bf16[4,8,384,128]{3,2,1,0:T(8,128)(2,1)S(1)} %bitcast.260, f32[4,8,64]{2,1,0:T(8,128)S(1)} %fusion.149, f32[4,8,64,384]{3,2,1,0:T(8,128)} %copy-done.1), kind=kOutput, calls=%fused_computation.49.clone.1 | convolution fusion | flops 203950464 | bytes 6823936 | tf_op jit(solution)/shard_map/while/body/eval_jaxpr/hnqk,hnkd->hnqd/dot_general | solution.py:36
  377.0 55.1 %all_to_all.78 = bf16[2,4,512,128]{3,1,0,2:T(4,128)(2,1)S(1)} all-to-all(bf16[2,4,512,128]{3,1,0,2:T(4,128)(2,1)} %get-tuple-element.188), channel_id=1, replica_groups=mesh['segment'=64,'fsdp'=8] {'fsdp'}, dimensions={2} | all-to-all | bytes 2097152 | tf_op jit(solution)/shard_map/all_to_all | solution.py:85
  432.1 3.2 copy.80
  435.3 4.2 convert_bitcast_fusion
  439.5 4.5 copy.81
  449.5 60.0 %collective-permute-done.1 = bf16[2,64,4096]{2,1,0:T(8,128)(2,1)S(1)} collective-permute-done((bf16[2,64,4096]{2,1,0:T(8,128)(2,1)S(1)}, bf16[2,64,4096]{2,1,0:T(8,128)(2,1)S(1)}, u32[]{:S(2)}, u32[]{:S(2)}) %collective-permute-start.1) | collective-permute-done | bytes 1048608 | tf_op jit(solution)/shard_map/ppermute | solution.py:13
  (123 shorter events, 86.7 us)
Async XLA Ops:
  3.8 14.3 %copy-start.8 = (bf16[2,1,16,32,32]{4,3,2,1,0:T(8,128)(2,1)S(1)}, bf16[2,1,16,32,32]{4,3,2,1,0:T(8,128)(2,1)}, u32[]{:S(2)}) copy-start(bf16[2,1,16,32,32]{4,3,2,1,0:T(8,128)(2,1)} %param.17) | copy-start | bytes 196612
  5.5 61.0 %all-to-all-start = ((bf16[2,64,32,128]{3,1,0,2:T(8,128)(2,1)}), bf16[2,64,32,128]{3,1,0,2:T(8,128)(2,1)S(1)}, u32[]{:S(2)}, u32[]{:S(2)}) async-start(bf16[2,64,32,128]{3,1,0,2:T(8,128)(2,1)} %copy.69), calls=%async_computation | async-start | bytes 2097152 | tf_op jit(solution)/shard_map/all_to_all | solution.py:83
  18.7 57.2 %copy-start.7 = (bf16[2,1,4,128,128]{4,3,2,1,0:T(8,128)(2,1)S(1)}, bf16[2,1,4,128,128]{4,3,2,1,0:T(8,128)(2,1)}, u32[]{:S(2)}) copy-start(bf16[2,1,4,128,128]{4,3,2,1,0:T(8,128)(2,1)} %param.14) | copy-start | bytes 786436
  18.7 57.2 %copy-start.9 = (s32[2,1,8,2]{2,3,1,0:T(2,128)S(1)}, s32[2,1,8,2]{2,3,1,0:T(2,128)}, u32[]{:S(2)}) copy-start(s32[2,1,8,2]{2,3,1,0:T(2,128)} %param.19) | copy-start | bytes 388
  66.5 66.0 %all-to-all-start.2 = ((bf16[8,2,16384]{2,1,0:T(2,128)(2,1)}), bf16[8,2,16384]{2,1,0:T(2,128)(2,1)}, u32[]{:S(2)}, u32[]{:S(2)}) async-start(bf16[8,2,16384]{2,1,0:T(2,128)(2,1)} %reshape.600), calls=%async_computation.2 | async-start | bytes 1048576 | tf_op jit(solution)/shard_map/all_to_all | solution.py:64
  76.0 66.4 %copy-start.10 = (s32[2,1]{0,1:T(1,128)S(1)}, s32[2,1]{0,1:T(1,128)}, u32[]{:S(2)}) copy-start(s32[2,1]{0,1:T(1,128)} %param.18) | copy-start | bytes 28
  86.0 1.7 copy-start
  114.3 1.7 copy-start
  132.5 57.9 %all-to-all-start.1 = ((bf16[2,4,512,128]{3,1,0,2:T(4,128)(2,1)}), bf16[2,4,512,128]{3,1,0,2:T(4,128)(2,1)S(1)}, u32[]{:S(2)}, u32[]{:S(2)}) async-start(bf16[2,4,512,128]{3,1,0,2:T(4,128)(2,1)} %get-tuple-element.187), calls=%async_computation.1 | async-start | bytes 2097152 | tf_op jit(solution)/shard_map/all_to_all | solution.py:85
  146.3 51.4 %copy-start.2 = (bf16[2,8,16,32,32]{3,4,2,1,0:T(8,128)(2,1)}, bf16[2,8,16,32,32]{3,4,2,1,0:T(8,128)(2,1)S(1)}, u32[]{:S(2)}) copy-start(bf16[2,8,16,32,32]{3,4,2,1,0:T(8,128)(2,1)S(1)} %copy.75) | copy-start | bytes 1572868
  203.0 1.9 copy-start.4
  206.3 51.9 %collective-permute-start = (bf16[2,64,4096]{2,1,0:T(8,128)(2,1)}, bf16[2,64,4096]{2,1,0:T(8,128)(2,1)S(1)}, u32[]{:S(2)}, u32[]{:S(2)}) collective-permute-start(bf16[2,64,4096]{2,1,0:T(8,128)(2,1)} %fusion.59), channel_id=1, source_target_pairs={{0,8},{8,16},{16,24},{24,32},{32,40},{40,48},{48,56},{56,64},{64,7... | collective-permute-start | bytes 3145736 | tf_op jit(solution)/shard_map/ppermute | solution.py:13
  258.7 1.0 copy-start.5
  261.1 57.0 %all-to-all-start.3 = ((bf16[2,64,32,128]{3,1,0,2:T(8,128)(2,1)}), bf16[2,64,32,128]{3,1,0,2:T(8,128)(2,1)S(1)}, u32[]{:S(2)}, u32[]{:S(2)}) async-start(bf16[2,64,32,128]{3,1,0,2:T(8,128)(2,1)} %copy_bitcast_fusion), calls=%async_computation.3 | async-start | bytes 2097152 | tf_op jit(solution)/shard_map/all_to_all | solution.py:83
  330.5 1.7 copy-start.1
  358.8 1.7 copy-start.1
  377.0 58.3 %copy-start.3 = (bf16[2,8,16,32,32]{3,4,2,1,0:T(8,128)(2,1)S(1)}, bf16[2,8,16,32,32]{3,4,2,1,0:T(8,128)(2,1)}, u32[]{:S(2)}) copy-start(bf16[2,8,16,32,32]{3,4,2,1,0:T(8,128)(2,1)} %copy-done.2) | copy-start | bytes 1572868
  444.0 1.6 copy-start.6
  447.5 61.9 %collective-permute-start.1 = (bf16[2,64,4096]{2,1,0:T(8,128)(2,1)S(1)}, bf16[2,64,4096]{2,1,0:T(8,128)(2,1)S(1)}, u32[]{:S(2)}, u32[]{:S(2)}) collective-permute-start(bf16[2,64,4096]{2,1,0:T(8,128)(2,1)S(1)} %fusion.58), channel_id=1, source_target_pairs={{0,8},{8,16},{16,24},{24,32},{32,40},{40,48},{48,56},{56,64},{64,7... | collective-permute-start | bytes 3145736 | tf_op jit(solution)/shard_map/ppermute | solution.py:13
